TPU v7x, 256 devices: a whole 4x4x8 slice. The times are simulated.
256 devices in a mesh: dp: 4 (over x), seq: 64 (over y, z, core).
Axes of the slice: x: 4, y: 4, z: 8, core: 2. Of those that a mesh axis runs over, the one named last changes fastest.
Arguments:
- tokens: bfloat16 [4, 8192, 2048], P('dp', 'seq'), may hold values from -6 to 6
- values: bfloat16 [4, 8192, 1024], P('dp', 'seq'), may hold values from -6 to 6
- cotangent: bfloat16 [4, 8192, 1024], P('dp', 'seq'), may hold values from -6 to 6
- sel_weight: bfloat16 [2048, 128], P(('dp', 'seq')), may hold values from -0.03125 to 0.03125
- step_weight: bfloat16 [2048, 32], P(('dp', 'seq')), may hold values from -0.125 to 0.125
- sel_dir: bfloat16 [2048, 128], P(('dp', 'seq')), may hold values from -0.03125 to 0.03125
- step_dir: bfloat16 [2048, 32], P(('dp', 'seq')), may hold values from -0.125 to 0.125
- conv_weight: float32 [4, 128], replicated, may hold values from -3 to 3
- step_bias: float32 [32], replicated, may hold values from -1 to 0.5
- decay_rate: float32 [32], replicated, may hold values from 0 to 1
Outputs:
- sel_grad: float32 [2048, 128], P(('dp', 'seq'))
- step_grad: float32 [2048, 32], P(('dp', 'seq'))
- sel_hvp: float32 [2048, 128], P(('dp', 'seq'))
- step_hvp: float32 [2048, 32], P(('dp', 'seq'))
All inputs are finite; a program needn't handle non-finite values.
Results may differ from a plain program's by a relative error of at most 0.0003.
Values may be sent and summed in bfloat16 or wider, within the bound.
A program may use at most 192 MiB of HBM per device.

v0:
```python
import math
import jax
import jax.numpy as jnp
from jax import lax
from jax.sharding import PartitionSpec as P

N = 64
P_SIZE = 32
H = 32
KCONV = 4
HIGHEST = lax.Precision.HIGHEST


def shifted(value, axis, steps):
    count = lax.axis_size(axis)
    initial, last = (max(0, -steps), min(count, count - steps))
    return lax.ppermute(value, axis, [(source, source + steps) for source in range(initial, last)])


def prefix(part, axis, combine, identity, reverse):
    count = lax.axis_size(axis)
    place = lax.axis_index(axis)
    ahead = count - 1 - place if reverse else place
    gathered = jax.tree.map(lambda a: lax.all_gather(a, axis), part)
    state = jax.tree.map(lambda a, e: jnp.zeros_like(a) + jnp.asarray(e, a.dtype), part, identity)

    def one(turn, state):
        source = count - 1 - turn if reverse else turn
        return combine(
            state, jax.tree.map(lambda a: lax.dynamic_index_in_dim(a, source, 0, False), gathered)
        )

    return lax.fori_loop(0, ahead, one, state)


def state_space(in_map, out_map, step_size, head_values, decay_rate, state_in):
    cumulated = jnp.cumsum(-step_size * decay_rate[None, :], axis=0)
    cumulated_heads = cumulated.T
    spans = cumulated_heads[:, :, None] - cumulated_heads[:, None, :]
    length = in_map.shape[0]
    causal = jnp.arange(length)[:, None] >= jnp.arange(length)[None, :]
    decays = jnp.exp(jnp.where(causal[None], spans, -1e30))
    intersection = jnp.dot(out_map, in_map.T, precision=HIGHEST)
    mixing = decays * intersection[None] * step_size.T[:, None, :]
    within = jnp.einsum("hts,shp->thp", mixing, head_values, precision=HIGHEST)
    carried = jnp.exp(cumulated)[:, :, None] * jnp.einsum(
        "tn,hpn->thp", out_map, state_in, precision=HIGHEST
    )
    whole_decay = cumulated[-1]
    tail_weight = jnp.exp(whole_decay[None, :] - cumulated) * step_size
    local_state = jnp.einsum(
        "thp,tn->hpn", head_values * tail_weight[:, :, None], in_map, precision=HIGHEST
    )
    state_out = jnp.exp(whole_decay)[:, None, None] * state_in + local_state
    return (within + carried, state_out)


def features(sel_float, step_float, extended, conv_weight, step_bias, length):
    projected = jnp.dot(extended, sel_float, precision=HIGHEST)
    convolved = conv_weight[0][None, :] * projected[0:length]
    for offset in range(1, KCONV):
        convolved = convolved + conv_weight[offset][None, :] * projected[offset : offset + length]
    activated = jax.nn.silu(convolved)
    step_size = jax.nn.softplus(
        jnp.dot(extended[KCONV - 1 :], step_float, precision=HIGHEST) + step_bias[None, :]
    )
    return (activated[:, :N], activated[:, N:], step_size)


def combine(earlier_segment, later_segment):
    decay_first, state_first, tangent_decay_first, tangent_state_first = earlier_segment
    decay_second, state_second, tangent_decay_second, tangent_state_second = later_segment
    combined_decay = decay_first * decay_second
    combined_state = decay_second[:, None, None] * state_first + state_second
    tangent_decay_combined = tangent_decay_first * decay_second + decay_first * tangent_decay_second
    tangent_state_combined = (
        tangent_decay_second[:, None, None] * state_first
        + decay_second[:, None, None] * tangent_state_first
        + tangent_state_second
    )
    return (combined_decay, combined_state, tangent_decay_combined, tangent_state_combined)


def body(
    tokens,
    values,
    cotangent,
    sel_weight,
    step_weight,
    sel_dir,
    step_dir,
    conv_weight,
    step_bias,
    decay_rate,
):
    own_tokens = tokens[0]
    length = own_tokens.shape[0]
    head_values = values[0].reshape(length, H, P_SIZE).astype(jnp.float32)
    head_cotangent = cotangent[0].reshape(length, H, P_SIZE).astype(jnp.float32)
    gathered = (
        lax.all_gather(sel_weight, ("dp", "seq"), axis=0, tiled=True),
        lax.all_gather(step_weight, ("dp", "seq"), axis=0, tiled=True),
        lax.all_gather(sel_dir, ("dp", "seq"), axis=0, tiled=True),
        lax.all_gather(step_dir, ("dp", "seq"), axis=0, tiled=True),
    )
    parameters = (gathered[0].astype(jnp.float32), gathered[1].astype(jnp.float32))
    directions = (gathered[2].astype(jnp.float32), gathered[3].astype(jnp.float32))
    previous = shifted(own_tokens[length - (KCONV - 1) :], "seq", 1)
    extended = jnp.concatenate([previous, own_tokens], axis=0).astype(jnp.float32)
    token_count = lax.axis_size("dp") * lax.axis_size("seq") * length
    scale_factor = 1.0 / math.sqrt(token_count)

    def summaries(weights):
        in_map, out_map, step_size = features(
            weights[0], weights[1], extended, conv_weight, step_bias, length
        )
        cumulated = jnp.cumsum(-step_size * decay_rate[None, :], axis=0)
        whole_decay = cumulated[-1]
        tail_weight = jnp.exp(whole_decay[None, :] - cumulated) * step_size
        local_state = jnp.einsum(
            "thp,tn->hpn", head_values * tail_weight[:, :, None], in_map, precision=HIGHEST
        )
        local_adjoint = scale_factor * jnp.einsum(
            "thp,tn->hpn",
            head_cotangent * jnp.exp(cumulated)[:, :, None],
            out_map,
            precision=HIGHEST,
        )
        return (jnp.exp(whole_decay), local_state, local_adjoint)

    primal, tangent = jax.jvp(summaries, (parameters,), (directions,))
    identity = (
        jnp.ones((H,), jnp.float32),
        jnp.zeros((H, P_SIZE, N), jnp.float32),
        jnp.zeros((H,), jnp.float32),
        jnp.zeros((H, P_SIZE, N), jnp.float32),
    )
    forward = prefix(
        (primal[0], primal[1], tangent[0], tangent[1]), "seq", combine, identity, False
    )
    backward = prefix(
        (primal[0], primal[2], tangent[0], tangent[2]), "seq", combine, identity, True
    )

    def objective(weights, state_start, end_adjoint):
        in_map, out_map, step_size = features(
            weights[0], weights[1], extended, conv_weight, step_bias, length
        )
        outputs, state_end = state_space(
            in_map, out_map, step_size, head_values, decay_rate, state_start
        )
        return scale_factor * jnp.sum(head_cotangent * outputs) + jnp.sum(end_adjoint * state_end)

    local_gradient = jax.grad(objective)
    gradients, curvature = jax.jvp(
        local_gradient, (parameters, forward[1], backward[1]), (directions, forward[3], backward[3])
    )
    reduced = (
        lax.psum_scatter(gradients[0], ("dp", "seq"), scatter_dimension=0, tiled=True),
        lax.psum_scatter(gradients[1], ("dp", "seq"), scatter_dimension=0, tiled=True),
        lax.psum_scatter(curvature[0], ("dp", "seq"), scatter_dimension=0, tiled=True),
        lax.psum_scatter(curvature[1], ("dp", "seq"), scatter_dimension=0, tiled=True),
    )
    return (reduced[0], reduced[1], reduced[2], reduced[3])


def solution(mesh):
    return jax.shard_map(
        body,
        mesh=mesh,
        in_specs=(
            P("dp", "seq", None),
            P("dp", "seq", None),
            P("dp", "seq", None),
            P(("dp", "seq"), None),
            P(("dp", "seq"), None),
            P(("dp", "seq"), None),
            P(("dp", "seq"), None),
            P(),
            P(),
            P(),
        ),
        out_specs=(
            P(("dp", "seq"), None),
            P(("dp", "seq"), None),
            P(("dp", "seq"), None),
            P(("dp", "seq"), None),
        ),
        check_vma=False,
    )
```

profile of v0, /device:TPU:8, one launch (start us, length us, event | category | flops | bytes accessed | tf_op | source)
XLA Modules:
  0.0 1398.3 jit_solution(11636096432629976415)
XLA Ops:
  8.1 1.9 collective-permute-start
  10.0 71.2 %all_gather.55 = bf16[2048,128]{1,0:T(8,128)(2,1)S(1)} all-gather(bf16[8,128]{1,0:T(8,128)(2,1)} %param.19), channel_id=1, replica_groups=mesh['dp'=4,'seq'=64] {'dp','seq'}, dimensions={0}, use_global_device_ids=true | all-gather | bytes 526336 | tf_op jit(solution)/shard_map/all_gather | solution.py:103
  81.2 65.5 %all_gather.50 = bf16[2048,128]{1,0:T(8,128)(2,1)S(1)} all-gather(bf16[8,128]{1,0:T(8,128)(2,1)} %param.17), channel_id=1, replica_groups=mesh['dp'=4,'seq'=64] {'dp','seq'}, dimensions={0}, use_global_device_ids=true | all-gather | bytes 526336 | tf_op jit(solution)/shard_map/all_gather | solution.py:101
  146.7 65.6 %all_gather.48 = bf16[2048,32]{1,0:T(8,128)(2,1)S(1)} all-gather(bf16[8,32]{1,0:T(8,128)(2,1)} %param.18), channel_id=1, replica_groups=mesh['dp'=4,'seq'=64] {'dp','seq'}, dimensions={0}, use_global_device_ids=true | all-gather | bytes 131584 | tf_op jit(solution)/shard_map/all_gather | solution.py:102
  212.3 65.5 %all_gather.53 = bf16[2048,32]{1,0:T(8,128)(2,1)S(1)} all-gather(bf16[8,32]{1,0:T(8,128)(2,1)} %param.20), channel_id=1, replica_groups=mesh['dp'=4,'seq'=64] {'dp','seq'}, dimensions={0}, use_global_device_ids=true | all-gather | bytes 131584 | tf_op jit(solution)/shard_map/all_gather | solution.py:104
  285.1 37.7 %all-gather.4 = f32[64,1,32]{2,1,0:T(1,128)S(1)} all-gather(f32[1,1,32]{2,1,0:T(1,128)S(1)} %get-tuple-element.315), channel_id=1, replica_groups=mesh['dp'=4,'seq'=64] {'seq'}, dimensions={0}, use_global_device_ids=true | all-gather | bytes 8320 | tf_op jit(solution)/shard_map/all_gather | solution.py:24
  322.8 38.1 %all-gather.5 = f32[64,1,32]{2,1,0:T(1,128)S(1)} all-gather(f32[1,1,32]{2,1,0:T(1,128)S(1)} %get-tuple-element.313), channel_id=1, replica_groups=mesh['dp'=4,'seq'=64] {'seq'}, dimensions={0}, use_global_device_ids=true | all-gather | bytes 8320 | tf_op jit(solution)/shard_map/all_gather | solution.py:24
  360.9 61.1 %all-gather.17.cloned.1.call-done = f32[2048,32,64]{2,1,0:T(8,128)} async-done(((f32[32,32,64]{2,1,0:T(8,128)}), f32[2048,32,64]{2,1,0:T(8,128)}) %all-gather.17.cloned.1.call-update) | async-done | bytes 16777232 | tf_op jit(solution)/shard_map/all_gather | solution.py:24
  422.0 142.3 %all-gather.15.cloned.1.call-done = f32[2048,32,64]{2,1,0:T(8,128)} async-done(((f32[32,32,64]{2,1,0:T(8,128)}), f32[2048,32,64]{2,1,0:T(8,128)}) %all-gather.15.cloned.1.call-update) | async-done | bytes 16777232 | tf_op jit(solution)/shard_map/all_gather | solution.py:24
  564.5 81.3 %while.33 = (s32[]{:T(128)}, f32[32,32,64]{2,1,0:T(8,128)S(1)}, f32[32,32,64]{2,1,0:T(8,128)S(1)}, s32[]{:T(128)}, f32[64,32]{1,0:T(8,128)S(1)}, /*index=5*/f32[...) while((s32[]{:T(128)}, f32[32,32,64]{2,1,0:T(8,128)S(1)}, ...), condition=%wide.region_6.7_spmd, body=%wide.region_5.6_spmd.sunk | while | flops 393222 | bytes 1573803 | solution.py:33
  564.5 1.7 bitcast_add_fusion.13
  566.2 1.7 bitcast_add_fusion.13
  568.0 1.7 bitcast_add_fusion.13
  569.7 1.7 bitcast_add_fusion.13
  571.4 1.7 bitcast_add_fusion.13
  573.1 1.7 bitcast_add_fusion.13
  574.9 1.7 bitcast_add_fusion.13
  576.6 1.7 bitcast_add_fusion.13
  578.3 1.7 bitcast_add_fusion.13
  580.0 1.7 bitcast_add_fusion.13
  581.8 1.7 bitcast_add_fusion.13
  583.5 1.7 bitcast_add_fusion.13
  585.2 1.7 bitcast_add_fusion.13
  586.9 1.7 bitcast_add_fusion.13
  588.7 1.7 bitcast_add_fusion.13
  590.4 1.7 bitcast_add_fusion.13
  592.1 1.7 bitcast_add_fusion.13
  593.8 1.7 bitcast_add_fusion.13
  595.6 1.7 bitcast_add_fusion.13
  597.3 1.7 bitcast_add_fusion.13
  600.8 1.7 bitcast_add_fusion.13
  604.2 1.7 bitcast_add_fusion.13
  612.8 1.7 bitcast_add_fusion.13
  616.3 1.7 bitcast_add_fusion.13
  619.7 1.7 bitcast_add_fusion.13
  623.2 1.7 bitcast_add_fusion.13
  626.6 1.7 bitcast_add_fusion.13
  630.1 1.7 bitcast_add_fusion.13
  633.5 1.7 bitcast_add_fusion.13
  637.0 1.7 bitcast_add_fusion.13
  655.5 5.9 fusion.150
  671.4 144.6 %all-gather.13.cloned.1.call-done = f32[2048,32,64]{2,1,0:T(8,128)} async-done(((f32[32,32,64]{2,1,0:T(8,128)}), f32[2048,32,64]{2,1,0:T(8,128)}) %all-gather.13.cloned.1.call-update) | async-done | bytes 16777232 | tf_op jit(solution)/shard_map/all_gather | solution.py:24
  816.0 142.2 %all-gather.11.cloned.1.call-done = f32[2048,32,64]{2,1,0:T(8,128)} async-done(((f32[32,32,64]{2,1,0:T(8,128)}), f32[2048,32,64]{2,1,0:T(8,128)}) %all-gather.11.cloned.1.call-update) | async-done | bytes 16777232 | tf_op jit(solution)/shard_map/all_gather | solution.py:24
  958.3 38.5 %while.32 = (s32[]{:T(128)}, f32[32,32,64]{2,1,0:T(8,128)S(1)}, f32[32,32,64]{2,1,0:T(8,128)S(1)}, s32[]{:T(128)}, f32[64,32]{1,0:T(8,128)}, /*index=5*/f32[64,3...) while((s32[]{:T(128)}, f32[32,32,64]{2,1,0:T(8,128)S(1)}, ...), condition=%wide.region_3.4_spmd, body=%wide.region_2.3_spmd.sunk | while | flops 393221 | bytes 1573783 | solution.py:33
  1001.1 1.8 convolution_bitcast_fusion.5
  1010.8 2.3 fusion.42
  1013.1 2.3 fusion.50
  1015.4 373.0 %all-reduce.21.cloned.1.call-done = (f32[2048,128]{1,0:T(8,128)}, f32[2048,32]{0,1:T(8,128)}, f32[2048,128]{1,0:T(8,128)}, f32[2048,32]{0,1:T(8,128)}) async-done(((f32[2048,128]{1,0:T(8,128)}, f32[2048,32]{0,1:T(8,128)}, f32[2048,128]{1,0:T(8,128)}, f32[2048,32]{0,1:T(8,128)}), (f32[2048,128]{1,0:T(8,128)}, f32[2048,32]{0,1:T(8,128)}, f32[2048,128]{1,0:T(8,128)}, ...) | async-done | bytes 2621456
  (281 shorter events, 109.8 us)
Async XLA Ops:
  7.2 270.6 %copy-start = (bf16[1,128,2048]{2,1,0:T(8,128)(2,1)S(1)}, bf16[1,128,2048]{2,1,0:T(8,128)(2,1)}, u32[]{:S(2)}) copy-start(bf16[1,128,2048]{2,1,0:T(8,128)(2,1)} %param.14) | copy-start | bytes 1572868
  7.2 270.6 %copy-start.46 = (f32[32]{0:T(128)S(1)}, f32[32]{0:T(128)}, u32[]{:S(2)}) copy-start(f32[32]{0:T(128)} %param.22) | copy-start | bytes 388
  7.2 270.9 %copy-start.29 = (f32[32]{0:T(128)S(1)}, f32[32]{0:T(128)}, u32[]{:S(2)}) copy-start(f32[32]{0:T(128)} %param.23) | copy-start | bytes 388
  7.2 414.8 %all-gather.17.cloned.1.call-start = ((), (), s32[]{:S(2)}) async-start(), calls=%async_computation.3 | async-start | bytes 34078720 | tf_op jit(solution)/shard_map/all_gather | solution.py:24
  8.1 271.7 %collective-permute-start = (bf16[3,2048]{1,0:T(4,128)(2,1)S(1)}, bf16[3,2048]{1,0:T(4,128)(2,1)S(1)}, u32[]{:S(2)}, u32[]{:S(2)}) collective-permute-start(bf16[3,2048]{1,0:T(4,128)(2,1)S(1)} %slice_bitcast_fusion), channel_id=1, source_target_pairs={{0,1},{1,2},{2,3},{3,4},{4,5},{5,6},{6,7},{7,8},{8,9},{9,10},{10,1... | collective-permute-start | bytes 36872 | tf_op jit(solution)/shard_map/ppermute | solution.py:17
  146.7 132.7 %copy-start.43 = (f32[4,128]{1,0:T(4,128)S(1)}, f32[4,128]{1,0:T(4,128)}, u32[]{:S(2)}) copy-start(f32[4,128]{1,0:T(4,128)} %param.21) | copy-start | bytes 6148
  146.7 132.8 %copy-start.12 = (bf16[1,128,1024]{2,1,0:T(8,128)(2,1)S(1)}, bf16[1,128,1024]{2,1,0:T(8,128)(2,1)}, u32[]{:S(2)}) copy-start(bf16[1,128,1024]{2,1,0:T(8,128)(2,1)} %param.16) | copy-start | bytes 786436
  278.4 375.1 %copy-start.1 = (f32[128,32]{1,0:T(8,128)}, f32[128,32]{1,0:T(8,128)S(1)}, u32[]{:S(2)}) copy-start(f32[128,32]{1,0:T(8,128)S(1)} %get-tuple-element.326) | copy-start | bytes 49156
  279.4 2.0 copy-start.8
  279.4 2.0 copy-start.33
  281.4 3.4 copy-start.10
  282.0 2.9 copy-start.15
  283.4 280.9 %all-gather.15.cloned.1.call-start = ((), (), s32[]{:S(2)}) async-start(), calls=%async_computation.2 | async-start | bytes 34078720 | tf_op jit(solution)/shard_map/all_gather | solution.py:24
  284.8 531.2 %all-gather.13.cloned.1.call-start = ((), (), s32[]{:S(2)}) async-start(), calls=%async_computation.1 | async-start | bytes 34078720 | tf_op jit(solution)/shard_map/all_gather | solution.py:24
  285.1 362.7 %copy-start.27 = (f32[32]{0:T(128)}, f32[32]{0:T(128)S(1)}, u32[]{:S(2)}) copy-start(f32[32]{0:T(128)S(1)} %get-tuple-element.314) | copy-start | bytes 388
  285.1 362.7 %copy-start.31 = (f32[32]{0:T(128)}, f32[32]{0:T(128)S(1)}, u32[]{:S(2)}) copy-start(f32[32]{0:T(128)S(1)} %get-tuple-element.312) | copy-start | bytes 388
  647.7 5.8 copy-start.5
  649.7 4.2 copy-start.13
  652.1 306.1 %all-gather.11.cloned.1.call-start = ((), (), s32[]{:S(2)}) async-start(), calls=%async_computation | async-start | bytes 34078720 | tf_op jit(solution)/shard_map/all_gather | solution.py:24
  653.5 734.9 %all-reduce.21.cloned.1.call-start = ((), (), s32[]{:S(2)}) async-start(), calls=%async_computation.4 | async-start | bytes 5242880
  661.4 296.8 %copy-start.3 = (f32[128,128]{1,0:T(8,128)}, f32[128,128]{1,0:T(8,128)S(1)}, u32[]{:S(2)}) copy-start(f32[128,128]{1,0:T(8,128)S(1)} %get-tuple-element.236) | copy-start | bytes 196612
  999.5 3.4 copy-start.41
  999.5 3.4 copy-start.42
  999.5 3.4 copy-start.44
  999.5 3.4 copy-start.45
  999.5 3.4 copy-start.9
  999.5 3.5 copy-start.17
  999.5 3.5 copy-start.18
  999.5 3.5 copy-start.19
  999.5 3.5 copy-start.20
  999.5 3.5 copy-start.21
  999.5 3.5 copy-start.28
  1001.1 4.3 copy-start.4
  1002.8 5.0 copy-start.7
  1002.8 5.0 copy-start.30
  1003.1 5.9 copy-start.2
  1003.1 5.9 copy-start.6
  1003.1 5.9 copy-start.14
  1003.1 5.9 copy-start.32
  1004.2 6.0 copy-start.24
  1004.2 6.3 copy-start.11
  1004.3 6.3 copy-start.16
  1004.3 6.3 copy-start.22
  1004.3 6.3 copy-start.23
  1004.3 6.3 copy-start.40
  1005.3 5.3 copy-start.34
  1005.3 5.3 copy-start.36
  1005.4 5.3 copy-start.38
  (5 other events, 7.6 us)
Sparse Core Ops, SparseCore 0:
  283.5 138.4 all-gather.16
  424.8 139.4 all-gather.14
  652.2 163.7 all-gather.12
  818.6 139.4 all-gather.10
  1015.6 372.8 all-reduce.20
where the time goes:
time: 1400 us
  waiting for transfers between devices  863 us (62%)
  blocking collectives  344 us (25%)
  other arithmetic  112 us (8%)
  matrix products  35.7 us (3%)
  local copies, waits for them, and re-layouts  24.1 us (2%)
  between operations  14.7 us (1%)
    all_gather x4, waiting for transfers between devices, prefix(): gathered = jax.tree.map(lambda a: lax.all_gather(a, axis), part)  490 us
    unnamed x6, waiting for transfers between devices  373 us
    add x63, other arithmetic, combine(): tangent_decay_second[:, None, None] * state_first  106 us
    all_gather x2, blocking collectives, prefix(): gathered = jax.tree.map(lambda a: lax.all_gather(a, axis), part)  75.8 us
    all_gather x1, blocking collectives, body(): lax.all_gather(sel_dir, ('dp', 'seq'), axis=0, tiled=True)  71.2 us
    all_gather x1, blocking collectives, body(): lax.all_gather(step_weight, ('dp', 'seq'), axis=0, tiled=True)  65.6 us
    all_gather x1, blocking collectives, body(): lax.all_gather(sel_weight, ('dp', 'seq'), axis=0, tiled=True)  65.5 us
    all_gather x1, blocking collectives, body(): lax.all_gather(step_dir, ('dp', 'seq'), axis=0, tiled=True)  65.5 us
  transfers between devices with their start and end apart: 6, of which 5 were waited for; matrix products, arithmetic and copies ran while one was open for 2% of the time, Pallas kernels for 0%

commit v1 on v0

--- a/solution.py
+++ b/solution.py
@@ -1,3 +1,4 @@
+import functools
 import math
 import jax
 import jax.numpy as jnp
@@ -9,6 +10,15 @@
 H = 32
 KCONV = 4
 HIGHEST = lax.Precision.HIGHEST
+
+
+def _fix_state(u_in, chip_axis):
+    value_now = jnp.stack([u_in for _ in range(lax.psum(1, chip_axis))])
+    w1 = lax.all_to_all(value_now, chip_axis, split_axis=0, concat_axis=0)
+    return jnp.concatenate(w1, 0)
+
+
+show_series_all = functools.partial(_fix_state, chip_axis=("dp", "seq"))
 
 
 def shifted(value, axis, steps):
@@ -99,7 +109,7 @@
     head_cotangent = cotangent[0].reshape(length, H, P_SIZE).astype(jnp.float32)
     gathered = (
         lax.all_gather(sel_weight, ("dp", "seq"), axis=0, tiled=True),
-        lax.all_gather(step_weight, ("dp", "seq"), axis=0, tiled=True),
+        show_series_all(step_weight),
         lax.all_gather(sel_dir, ("dp", "seq"), axis=0, tiled=True),
         lax.all_gather(step_dir, ("dp", "seq"), axis=0, tiled=True),
     )

time: 1400 us -> 1350 us (0.964)
  blocking collectives: 344 us -> 277 us
  starting transfers between devices: 2.13 us -> 17.5 us
    all_gather x1 -> x0, blocking collectives: 65.6 us -> none  [body(): lax.all_gather(step_weight, ('dp', 'seq'), axis=0, tiled=True)]
    all_to_all x0 -> x1, starting transfers between devices: none -> 15.3 us  [_fix_state(): w1 = lax.all_to_all(value_now, chip_axis, split_axis=0, concat_axis=0)]
  transfers between devices with their start and end apart: 6 -> 7, of which waited for: 5 -> 5; matrix products, arithmetic and copies ran while one was open for 2% -> 2% of each run, Pallas kernels for 0% -> 0%
where the time goes in v1:
time: 1350 us
  waiting for transfers between devices  864 us (64%)
  blocking collectives  277 us (21%)
  other arithmetic  112 us (8%)
  matrix products  35.8 us (3%)
  local copies, waits for them, and re-layouts  26 us (2%)
  starting transfers between devices  17.5 us (1%)
  between operations  14.7 us (1%)
    all_gather x4, waiting for transfers between devices, prefix(): gathered = jax.tree.map(lambda a: lax.all_gather(a, axis), part)  491 us
    unnamed x6, waiting for transfers between devices  373 us
    add x63, other arithmetic, combine(): tangent_decay_second[:, None, None] * state_first  106 us
    all_gather x2, blocking collectives, prefix(): gathered = jax.tree.map(lambda a: lax.all_gather(a, axis), part)  75.8 us
    all_gather x1, blocking collectives, body(): lax.all_gather(sel_dir, ('dp', 'seq'), axis=0, tiled=True)  69.7 us
    all_gather x1, blocking collectives, body(): lax.all_gather(step_dir, ('dp', 'seq'), axis=0, tiled=True)  65.6 us
    all_gather x1, blocking collectives, body(): lax.all_gather(sel_weight, ('dp', 'seq'), axis=0, tiled=True)  65.5 us
  transfers between devices with their start and end apart: 7, of which 5 were waited for; matrix products, arithmetic and copies ran while one was open for 2% of the time, Pallas kernels for 0%

profile of v1, /device:TPU:8, one launch (start us, length us, event | category | flops | bytes accessed | tf_op | source)
XLA Modules:
  0.0 1348.8 jit_solution(12054182434155826631)
XLA Ops:
  8.0 1.9 collective-permute-start
  11.7 15.3 %all-to-all-start = ((bf16[256,2,128]{2,1,0:T(2,128)(2,1)}), bf16[256,2,128]{2,1,0:T(2,128)(2,1)S(1)}, u32[]{:S(2)}, u32[]{:S(2)}) async-start(bf16[256,2,128]{2,1,0:T(2,128)(2,1)} %reshape.135), calls=%async_computation | async-start | bytes 262144 | tf_op jit(solution)/shard_map/all_to_all | solution.py:17
  27.0 69.7 %all_gather.51 = bf16[2048,128]{1,0:T(8,128)(2,1)S(1)} all-gather(bf16[8,128]{1,0:T(8,128)(2,1)} %param.19), channel_id=1, replica_groups=mesh['dp'=4,'seq'=64] {'dp','seq'}, dimensions={0}, use_global_device_ids=true | all-gather | bytes 526336 | tf_op jit(solution)/shard_map/all_gather | solution.py:113
  96.7 65.5 %all_gather.46 = bf16[2048,128]{1,0:T(8,128)(2,1)S(1)} all-gather(bf16[8,128]{1,0:T(8,128)(2,1)} %param.17), channel_id=1, replica_groups=mesh['dp'=4,'seq'=64] {'dp','seq'}, dimensions={0}, use_global_device_ids=true | all-gather | bytes 526336 | tf_op jit(solution)/shard_map/all_gather | solution.py:111
  162.3 65.6 %all_gather.49 = bf16[2048,32]{1,0:T(8,128)(2,1)S(1)} all-gather(bf16[8,32]{1,0:T(8,128)(2,1)S(1)} %copy-done.40), channel_id=1, replica_groups=mesh['dp'=4,'seq'=64] {'dp','seq'}, dimensions={0}, use_global_device_ids=true | all-gather | bytes 131584 | tf_op jit(solution)/shard_map/all_gather | solution.py:114
  234.9 38.1 %all-gather.4 = f32[64,1,32]{2,1,0:T(1,128)S(1)} all-gather(f32[1,1,32]{2,1,0:T(1,128)S(1)} %get-tuple-element.315), channel_id=1, replica_groups=mesh['dp'=4,'seq'=64] {'seq'}, dimensions={0}, use_global_device_ids=true | all-gather | bytes 8320 | tf_op jit(solution)/shard_map/all_gather | solution.py:34
  273.0 37.6 %all-gather.5 = f32[64,1,32]{2,1,0:T(1,128)S(1)} all-gather(f32[1,1,32]{2,1,0:T(1,128)S(1)} %get-tuple-element.313), channel_id=1, replica_groups=mesh['dp'=4,'seq'=64] {'seq'}, dimensions={0}, use_global_device_ids=true | all-gather | bytes 8320 | tf_op jit(solution)/shard_map/all_gather | solution.py:34
  310.7 61.5 %all-gather.17.cloned.1.call-done = f32[2048,32,64]{2,1,0:T(8,128)} async-done(((f32[32,32,64]{2,1,0:T(8,128)}), f32[2048,32,64]{2,1,0:T(8,128)}) %all-gather.17.cloned.1.call-update) | async-done | bytes 16777232 | tf_op jit(solution)/shard_map/all_gather | solution.py:34
  372.2 142.3 %all-gather.15.cloned.1.call-done = f32[2048,32,64]{2,1,0:T(8,128)} async-done(((f32[32,32,64]{2,1,0:T(8,128)}), f32[2048,32,64]{2,1,0:T(8,128)}) %all-gather.15.cloned.1.call-update) | async-done | bytes 16777232 | tf_op jit(solution)/shard_map/all_gather | solution.py:34
  514.7 81.3 %while.33 = (s32[]{:T(128)}, f32[32,32,64]{2,1,0:T(8,128)S(1)}, f32[32,32,64]{2,1,0:T(8,128)S(1)}, s32[]{:T(128)}, f32[64,32]{1,0:T(8,128)S(1)}, /*index=5*/f32[...) while((s32[]{:T(128)}, f32[32,32,64]{2,1,0:T(8,128)S(1)}, ...), condition=%wide.region_6.7_spmd, body=%wide.region_5.6_spmd.sunk | while | flops 393222 | bytes 1573803 | solution.py:43
  514.7 1.7 bitcast_add_fusion.13
  516.4 1.7 bitcast_add_fusion.13
  518.2 1.7 bitcast_add_fusion.13
  519.9 1.7 bitcast_add_fusion.13
  521.6 1.7 bitcast_add_fusion.13
  523.3 1.7 bitcast_add_fusion.13
  525.1 1.7 bitcast_add_fusion.13
  526.8 1.7 bitcast_add_fusion.13
  528.5 1.7 bitcast_add_fusion.13
  530.2 1.7 bitcast_add_fusion.13
  532.0 1.7 bitcast_add_fusion.13
  533.7 1.7 bitcast_add_fusion.13
  535.4 1.7 bitcast_add_fusion.13
  537.1 1.7 bitcast_add_fusion.13
  538.9 1.7 bitcast_add_fusion.13
  540.6 1.7 bitcast_add_fusion.13
  542.3 1.7 bitcast_add_fusion.13
  544.0 1.7 bitcast_add_fusion.13
  545.8 1.7 bitcast_add_fusion.13
  554.4 1.7 bitcast_add_fusion.13
  557.9 1.7 bitcast_add_fusion.13
  561.3 1.7 bitcast_add_fusion.13
  564.8 1.7 bitcast_add_fusion.13
  568.2 1.7 bitcast_add_fusion.13
  571.7 1.7 bitcast_add_fusion.13
  575.1 1.7 bitcast_add_fusion.13
  578.6 1.7 bitcast_add_fusion.13
  587.2 1.7 bitcast_add_fusion.13
  590.6 1.7 bitcast_add_fusion.13
  594.1 1.7 bitcast_add_fusion.13
  605.0 5.9 fusion.151
  621.6 144.6 %all-gather.13.cloned.1.call-done = f32[2048,32,64]{2,1,0:T(8,128)} async-done(((f32[32,32,64]{2,1,0:T(8,128)}), f32[2048,32,64]{2,1,0:T(8,128)}) %all-gather.13.cloned.1.call-update) | async-done | bytes 16777232 | tf_op jit(solution)/shard_map/all_gather | solution.py:34
  766.2 142.2 %all-gather.11.cloned.1.call-done = f32[2048,32,64]{2,1,0:T(8,128)} async-done(((f32[32,32,64]{2,1,0:T(8,128)}), f32[2048,32,64]{2,1,0:T(8,128)}) %all-gather.11.cloned.1.call-update) | async-done | bytes 16777232 | tf_op jit(solution)/shard_map/all_gather | solution.py:34
  908.5 38.5 %while.32 = (s32[]{:T(128)}, f32[32,32,64]{2,1,0:T(8,128)S(1)}, f32[32,32,64]{2,1,0:T(8,128)S(1)}, s32[]{:T(128)}, f32[64,32]{1,0:T(8,128)}, /*index=5*/f32[64,3...) while((s32[]{:T(128)}, f32[32,32,64]{2,1,0:T(8,128)S(1)}, ...), condition=%wide.region_3.4_spmd, body=%wide.region_2.3_spmd.sunk | while | flops 393221 | bytes 1573783 | solution.py:43
  951.2 1.8 convolution_bitcast_fusion.5
  961.0 2.3 fusion.43
  963.3 2.3 fusion.51
  965.6 373.2 %all-reduce.21.cloned.1.call-done = (f32[2048,128]{1,0:T(8,128)}, f32[2048,32]{0,1:T(8,128)}, f32[2048,128]{1,0:T(8,128)}, f32[2048,32]{0,1:T(8,128)}) async-done(((f32[2048,128]{1,0:T(8,128)}, f32[2048,32]{0,1:T(8,128)}, f32[2048,128]{1,0:T(8,128)}, f32[2048,32]{0,1:T(8,128)}), (f32[2048,128]{1,0:T(8,128)}, f32[2048,32]{0,1:T(8,128)}, f32[2048,128]{1,0:T(8,128)}, ...) | async-done | bytes 2621456
  (285 shorter events, 111.1 us)
Async XLA Ops:
  7.2 220.9 %copy-start = (bf16[1,128,2048]{2,1,0:T(8,128)(2,1)S(1)}, bf16[1,128,2048]{2,1,0:T(8,128)(2,1)}, u32[]{:S(2)}) copy-start(bf16[1,128,2048]{2,1,0:T(8,128)(2,1)} %param.14) | copy-start | bytes 1572868
  7.2 155.0 %copy-start.43 = (f32[4,128]{1,0:T(4,128)S(1)}, f32[4,128]{1,0:T(4,128)}, u32[]{:S(2)}) copy-start(f32[4,128]{1,0:T(4,128)} %param.21) | copy-start | bytes 6148
  7.2 155.0 %copy-start.40 = (bf16[8,32]{1,0:T(8,128)(2,1)S(1)}, bf16[8,32]{1,0:T(8,128)(2,1)}, u32[]{:S(2)}) copy-start(bf16[8,32]{1,0:T(8,128)(2,1)} %param.20) | copy-start | bytes 1540
  7.2 220.7 %copy-start.12 = (bf16[1,128,1024]{2,1,0:T(8,128)(2,1)S(1)}, bf16[1,128,1024]{2,1,0:T(8,128)(2,1)}, u32[]{:S(2)}) copy-start(bf16[1,128,1024]{2,1,0:T(8,128)(2,1)} %param.16) | copy-start | bytes 786436
  8.0 220.0 %collective-permute-start = (bf16[3,2048]{1,0:T(4,128)(2,1)S(1)}, bf16[3,2048]{1,0:T(4,128)(2,1)S(1)}, u32[]{:S(2)}, u32[]{:S(2)}) collective-permute-start(bf16[3,2048]{1,0:T(4,128)(2,1)S(1)} %slice_bitcast_fusion), channel_id=1, source_target_pairs={{0,1},{1,2},{2,3},{3,4},{4,5},{5,6},{6,7},{7,8},{8,9},{9,10},{10,1... | collective-permute-start | bytes 36872 | tf_op jit(solution)/shard_map/ppermute | solution.py:27
  11.7 218.1 %all-to-all-start = ((bf16[256,2,128]{2,1,0:T(2,128)(2,1)}), bf16[256,2,128]{2,1,0:T(2,128)(2,1)S(1)}, u32[]{:S(2)}, u32[]{:S(2)}) async-start(bf16[256,2,128]{2,1,0:T(2,128)(2,1)} %reshape.135), calls=%async_computation | async-start | bytes 262144 | tf_op jit(solution)/shard_map/all_to_all | solution.py:17
  27.0 345.2 %all-gather.17.cloned.1.call-start = ((), (), s32[]{:S(2)}) async-start(), calls=%async_computation.4 | async-start | bytes 34078720 | tf_op jit(solution)/shard_map/all_gather | solution.py:34
  162.2 66.6 %copy-start.32 = (f32[128]{0:T(128)}, f32[128]{0:T(128)S(1)}, u32[]{:S(2)}) copy-start(f32[128]{0:T(128)S(1)} %get-tuple-element.319) | copy-start | bytes 1540
  162.2 66.6 %copy-start.34 = (f32[128]{0:T(128)}, f32[128]{0:T(128)S(1)}, u32[]{:S(2)}) copy-start(f32[128]{0:T(128)S(1)} %get-tuple-element.321) | copy-start | bytes 1540
  162.2 66.6 %copy-start.36 = (f32[128]{0:T(128)}, f32[128]{0:T(128)S(1)}, u32[]{:S(2)}) copy-start(f32[128]{0:T(128)S(1)} %get-tuple-element.322) | copy-start | bytes 1540
  162.3 66.6 %copy-start.38 = (f32[128]{0:T(128)}, f32[128]{0:T(128)S(1)}, u32[]{:S(2)}) copy-start(f32[128]{0:T(128)S(1)} %get-tuple-element.320) | copy-start | bytes 1540
  230.7 373.9 %copy-start.1 = (f32[128,32]{1,0:T(8,128)}, f32[128,32]{1,0:T(8,128)S(1)}, u32[]{:S(2)}) copy-start(f32[128,32]{1,0:T(8,128)S(1)} %get-tuple-element.326) | copy-start | bytes 49156
  231.0 3.6 copy-start.8
  233.2 281.4 %all-gather.15.cloned.1.call-start = ((), (), s32[]{:S(2)}) async-start(), calls=%async_computation.3 | async-start | bytes 34078720 | tf_op jit(solution)/shard_map/all_gather | solution.py:34
  234.6 531.5 %all-gather.13.cloned.1.call-start = ((), (), s32[]{:S(2)}) async-start(), calls=%async_computation.2 | async-start | bytes 34078720 | tf_op jit(solution)/shard_map/all_gather | solution.py:34
  234.9 363.1 %copy-start.26 = (f32[32]{0:T(128)}, f32[32]{0:T(128)S(1)}, u32[]{:S(2)}) copy-start(f32[32]{0:T(128)S(1)} %get-tuple-element.314) | copy-start | bytes 388
  234.9 363.1 %copy-start.30 = (f32[32]{0:T(128)}, f32[32]{0:T(128)S(1)}, u32[]{:S(2)}) copy-start(f32[32]{0:T(128)S(1)} %get-tuple-element.312) | copy-start | bytes 388
  597.9 5.8 copy-start.5
  602.2 306.1 %all-gather.11.cloned.1.call-start = ((), (), s32[]{:S(2)}) async-start(), calls=%async_computation.1 | async-start | bytes 34078720 | tf_op jit(solution)/shard_map/all_gather | solution.py:34
  603.6 735.2 %all-reduce.21.cloned.1.call-start = ((), (), s32[]{:S(2)}) async-start(), calls=%async_computation.5 | async-start | bytes 5242880
  610.9 297.5 %copy-start.3 = (f32[128,128]{1,0:T(8,128)}, f32[128,128]{1,0:T(8,128)S(1)}, u32[]{:S(2)}) copy-start(f32[128,128]{1,0:T(8,128)S(1)} %get-tuple-element.236) | copy-start | bytes 196612
  949.6 3.4 copy-start.41
  949.6 3.4 copy-start.42
  949.7 3.4 copy-start.44
  949.7 3.4 copy-start.45
  949.7 3.4 copy-start.9
  949.7 3.4 copy-start.16
  949.7 3.4 copy-start.17
  949.7 3.4 copy-start.18
  949.7 3.4 copy-start.19
  949.7 3.4 copy-start.20
  949.7 3.4 copy-start.27
  951.2 4.3 copy-start.4
  953.0 5.0 copy-start.7
  953.0 5.0 copy-start.29
  953.3 5.9 copy-start.2
  953.3 5.9 copy-start.6
  953.3 5.9 copy-start.13
  953.3 5.9 copy-start.31
  954.4 6.0 copy-start.23
  954.4 6.3 copy-start.11
  954.4 6.3 copy-start.15
  954.4 6.3 copy-start.21
  954.5 6.3 copy-start.22
  954.5 6.3 copy-start.39
  955.5 5.3 copy-start.33
  955.5 5.3 copy-start.35
  955.5 5.3 copy-start.37
  (6 other events, 10.0 us)
Sparse Core Ops, SparseCore 0:
  233.3 138.8 all-gather.16
  375.0 139.4 all-gather.14
  602.3 163.8 all-gather.12
  768.8 139.4 all-gather.10
  965.7 373.0 all-reduce.20
